TPU v7x, 256 devices: a whole 4x4x8 slice. The times are simulated.
256 devices in a mesh: role: 2 (over core), slot: 32 (over z, x), tp: 4 (over y).
Axes of the slice: x: 4, y: 4, z: 8, core: 2. Of those that a mesh axis runs over, the one named last changes fastest.
Arguments:
- queries: bfloat16 [2, 8192, 8192], P('role', 'slot', 'tp'), may hold values from -16 to 16
- cache_keys: bfloat16 [2, 256, 8, 256, 128], P('role', 'slot', 'tp'), may hold values from -16 to 16
- cache_values: bfloat16 [2, 256, 8, 256, 128], P('role', 'slot', 'tp'), may hold values from -6 to 6
- new_keys: bfloat16 [2, 8192, 1024], P('role', 'slot', 'tp'), may hold values from -16 to 16
- new_values: bfloat16 [2, 8192, 1024], P('role', 'slot', 'tp'), may hold values from -6 to 6
- out_weight: bfloat16 [2, 8192, 8192], P('role', 'tp'), may hold values from -0.0625 to 0.0625
- fork_src: int32 [256], P(('role', 'slot')), may hold values from 0 to 255, as said below
- cache_blocks: int32 [256], P('slot'), may hold values from 1 to 2, 320 in all
Outputs:
- layer_out: bfloat16 [2, 8192, 8192], P('role', ('slot', 'tp'))
Inputs may be any that keep to these rules, and one draw needn't show every extreme that they name: For every index a < 32, exactly 2 of the slots j with j // 8 = a have fork_src[j] = j (survivors); every other entry names a survivor. For all a and b, at most 1 slots j with j // 8 = a and fork_src[j] != j have fork_src[j] // 8 = b, and for every a some b has exactly 1.
All inputs are finite; a program needn't handle non-finite values. No bound on the sum of `cache_blocks` on one device may be relied on, other than what follows from the above.
Results may differ from a plain program's by a relative error of at most 0.0095.
Values may be sent and summed in bfloat16 or wider, within the bound.
No kernel may reach another device: no remote copies, remote signals or barrier semaphores. Data moves between devices by JAX's collectives and lax.ppermute only.
A program may use at most 128 MiB of HBM per device.

v0:
```python
import jax
import jax.numpy as jnp
from jax import lax
from jax.sharding import PartitionSpec as P

BLK = 128


def partial_softmax(query_matrix_rows, key_matrix_rows, value_matrix_rows, allowed, logit_scale):
    attention_logits = (
        jnp.einsum(
            "syu,swu->syw", query_matrix_rows, key_matrix_rows, preferred_element_type=jnp.float32
        )
        * logit_scale
    )
    attention_logits = jnp.where(allowed[None], attention_logits, -jnp.inf)
    part_max = jnp.max(attention_logits, axis=-1)
    softmax_weights = jnp.exp(attention_logits - part_max[..., None])
    part_sum = jnp.sum(softmax_weights, axis=-1)
    partial_output = jnp.einsum(
        "fzo,fol->fzl",
        softmax_weights.astype(jnp.bfloat16),
        value_matrix_rows,
        preferred_element_type=jnp.float32,
    )
    return (partial_output, part_max, part_sum)


def normalise(part):
    partial_output, part_max, part_sum = part
    return ((partial_output / part_sum[..., None]).astype(jnp.bfloat16), part_max, part_sum)


def combine(cache_part, step_part):
    cache_att, cache_max, cache_sum = cache_part
    step_out, step_max, step_sum = step_part
    cache_float = lax.optimization_barrier(cache_att).astype(jnp.float32)
    joint_max = jnp.maximum(cache_max, step_max)
    cache_weight = jnp.exp(cache_max - joint_max) * cache_sum
    step_scale = jnp.exp(step_max - joint_max)
    numer = cache_float * cache_weight[..., None] + step_out * step_scale[..., None]
    denom = cache_weight + step_sum * step_scale
    return (numer / denom[..., None]).astype(jnp.bfloat16)


def shards(
    queries, cache_keys, cache_values, new_keys, new_values, out_weight, fork_src, cache_blocks
):
    slot_count = lax.axis_size("slot")
    slot_here = lax.axis_index("slot")
    node_dev = cache_keys.shape[1]
    kv_heads = cache_keys.shape[2]
    token_cap = cache_keys.shape[3]
    head_dim = cache_keys.shape[4]
    step_rows = queries.shape[1] // node_dev
    group_size = queries.shape[2] // (head_dim * kv_heads)
    logit_scale = float(head_dim) ** (-0.5)
    block_len = BLK
    fork_cap = (node_dev - node_dev // 4 + slot_count - 1) // slot_count
    buffer_total = slot_count * fork_cap
    parents = lax.all_gather(fork_src, ("role", "slot"), axis=0, tiled=True)
    node_ids = jnp.arange(parents.shape[0], dtype=jnp.int32)
    moving_all = parents != node_ids
    source_dev = parents // node_dev
    local_ids = jnp.arange(node_dev, dtype=jnp.int32)
    own_parents = lax.dynamic_slice_in_dim(parents, slot_here * node_dev, node_dev)
    own_moving = own_parents != slot_here * node_dev + local_ids
    own_source = own_parents // node_dev
    earlier = (
        (own_source[:, None] == own_source[None, :])
        & own_moving[None, :]
        & (local_ids[None, :] < local_ids[:, None])
    )
    recv_rank = jnp.sum(earlier.astype(jnp.int32), axis=1)
    recv_slot = jnp.minimum(own_source * fork_cap + recv_rank, buffer_total - 1)
    from_here = (moving_all & (source_dev == slot_here)).reshape(slot_count, node_dev)
    send_rank = jnp.cumsum(from_here.astype(jnp.int32), axis=1) - 1
    parent_local = (parents % node_dev).reshape(slot_count, node_dev)
    rank_ids = jnp.arange(fork_cap, dtype=jnp.int32)
    matches = from_here[:, None, :] & (send_rank[:, None, :] == rank_ids[None, :, None])
    send_node = jnp.sum(jnp.where(matches, parent_local[:, None, :], 0), axis=2).reshape(
        buffer_total
    )
    query_nodes = (
        queries[0]
        .reshape(node_dev, step_rows, kv_heads, group_size, head_dim)
        .transpose(0, 2, 1, 3, 4)
        .reshape(node_dev, kv_heads, step_rows * group_size, head_dim)
    )
    step_keys = new_keys[0].reshape(node_dev, step_rows, kv_heads, head_dim).transpose(0, 2, 1, 3)
    step_values = (
        new_values[0].reshape(node_dev, step_rows, kv_heads, head_dim).transpose(0, 2, 1, 3)
    )
    row_step = jnp.arange(step_rows * group_size) // group_size
    causal = jnp.arange(step_rows)[None, :] <= row_step[:, None]
    step_parts = jax.vmap(
        lambda query_matrix_rows, key_matrix_rows, value_matrix_rows: partial_softmax(
            query_matrix_rows, key_matrix_rows, value_matrix_rows, causal, logit_scale
        )
    )(query_nodes, step_keys, step_values)
    send_keys = cache_keys[0][send_node]
    send_values = cache_values[0][send_node]
    send_blocks = cache_blocks[send_node]
    fetched_keys, fetched_values, fetched_blocks = (
        lax.all_to_all(send_keys, "slot", split_axis=0, concat_axis=0, tiled=True),
        lax.all_to_all(send_values, "slot", split_axis=0, concat_axis=0, tiled=True),
        lax.all_to_all(send_blocks, "slot", split_axis=0, concat_axis=0, tiled=True),
    )
    fork_blocks = jnp.where(own_moving, fetched_blocks[recv_slot], cache_blocks)

    def attend_node(node_index):
        moving = own_moving[node_index]
        buffer_pos = recv_slot[node_index]
        key_matrix_rows = jnp.where(moving, fetched_keys[buffer_pos], cache_keys[0, node_index])
        value_matrix_rows = jnp.where(
            moving, fetched_values[buffer_pos], cache_values[0, node_index]
        )
        allowed = (jnp.arange(token_cap) < fork_blocks[node_index] * block_len)[None, :]
        return normalise(
            partial_softmax(
                query_nodes[node_index], key_matrix_rows, value_matrix_rows, allowed, logit_scale
            )
        )

    cache_parts = lax.map(attend_node, local_ids)
    attention = combine(cache_parts, step_parts)
    attention = (
        attention.reshape(node_dev, kv_heads, step_rows, group_size, head_dim)
        .transpose(0, 2, 1, 3, 4)
        .reshape(node_dev * step_rows, kv_heads * group_size * head_dim)
    )
    summed = lax.psum_scatter(
        jnp.dot(attention, out_weight[0], preferred_element_type=jnp.float32).astype(jnp.bfloat16),
        "tp",
        scatter_dimension=0,
        tiled=True,
    )
    return summed[None]


def solution(mesh):
    in_specs = (
        P("role", "slot", "tp"),
        P("role", "slot", "tp", None, None),
        P("role", "slot", "tp", None, None),
        P("role", "slot", "tp"),
        P("role", "slot", "tp"),
        P("role", "tp", None),
        P(("role", "slot")),
        P("slot"),
    )
    out_specs = P("role", ("slot", "tp"), None)
    return jax.shard_map(shards, mesh=mesh, in_specs=in_specs, out_specs=out_specs, check_vma=False)
```

profile of v0, /device:TPU:102, one launch (start us, length us, event | category | flops | bytes accessed | tf_op | source)
XLA Modules:
  0.0 419.8 jit_solution(10146846277897787751)
XLA Ops:
  6.5 1.3 dynamic-slice
  9.3 19.9 %all-reduce = s32[256]{0:T(256)S(1)} all-reduce(s32[256]{0:T(256)S(1)} %dynamic-update-slice), channel_id=1, replica_groups=mesh['role'=2,'slot'=32,'tp'=4] {'role','slot'}, use_global_device_ids=true, to_apply=%add | all-reduce | flops 256 | bytes 2048
  29.7 1.4 gather_fusion
  31.8 7.4 %all-to-all-start = ((s32[32,1,1]{2,1,0:T(1,128)}), s32[32,1,1]{2,1,0:T(1,128)S(1)}, u32[]{:S(2)}, u32[]{:S(2)}) async-start(s32[32,1,1]{2,1,0:T(1,128)} %copy.31), calls=%async_computation | async-start | bytes 32768 | tf_op jit(solution)/shard_map/all_to_all | solution.py:107
  39.1 4.3 %gather_fusion.2 = bf16[32,2,256,128]{3,2,1,0:T(8,128)(2,1)} fusion(bf16[8,2,256,128]{3,2,1,0:T(8,128)(2,1)} %bitcast.108, s32[1024]{0:T(1024)S(1)} %pad_clamp_fusion.1), kind=kCustom, calls=%fused_computation.2 | custom fusion | bytes 8388736 | tf_op jit(solution)/shard_map/gather | solution.py:101
  43.4 1.0 all-to-all-done
  44.4 9.1 %all-to-all-start.1 = ((bf16[32,2,256,128]{3,2,1,0:T(8,128)(2,1)}), bf16[32,2,256,128]{3,2,1,0:T(8,128)(2,1)}, u32[]{:S(2)}, u32[]{:S(2)}) async-start(bf16[32,2,256,128]{3,2,1,0:T(8,128)(2,1)} %gather_fusion.2), calls=%async_computation.1 | async-start | bytes 8388608 | tf_op jit(solution)/shard_map/all_to_all | solution.py:105
  53.6 3.1 gather_fusion.3
  56.7 90.4 %all-to-all-done.1 = bf16[32,2,256,128]{3,2,1,0:T(8,128)(2,1)} async-done(((bf16[32,2,256,128]{3,2,1,0:T(8,128)(2,1)}), bf16[32,2,256,128]{3,2,1,0:T(8,128)(2,1)}, u32[]{:S(2)}, u32[]{:S(2)}) %all-to-all-start.1) | async-done | bytes 4194336 | tf_op jit(solution)/shard_map/all_to_all | solution.py:105
  147.0 7.6 %all-to-all-start.2 = ((bf16[32,2,256,128]{3,2,1,0:T(8,128)(2,1)}), bf16[32,2,256,128]{3,2,1,0:T(8,128)(2,1)}, u32[]{:S(2)}, u32[]{:S(2)}) async-start(bf16[32,2,256,128]{3,2,1,0:T(8,128)(2,1)} %gather_fusion.3), calls=%async_computation.2 | async-start | bytes 8388608 | tf_op jit(solution)/shard_map/all_to_all | solution.py:106
  157.5 1.4 reduce.1
  159.6 89.1 %all-to-all-done.2 = bf16[32,2,256,128]{3,2,1,0:T(8,128)(2,1)} async-done(((bf16[32,2,256,128]{3,2,1,0:T(8,128)(2,1)}), bf16[32,2,256,128]{3,2,1,0:T(8,128)(2,1)}, u32[]{:S(2)}, u32[]{:S(2)}) %all-to-all-start.2) | async-done | bytes 4194336 | tf_op jit(solution)/shard_map/all_to_all | solution.py:106
  248.8 94.0 %while.14 = (s32[]{:T(128)}, bf16[8,2,256,128]{3,2,1,0:T(8,128)(2,1)}, f32[8,2,256]{2,1,0:T(2,128)}, f32[8,2,256]{2,1,0:T(2,128)}, s32[8]{0:T(128)S(1)}, /*index...) while((s32[]{:T(128)}, ...), condition=%wide.region_6.7_spmd, body=%wide.region_3.6_spmd.sunk | while | flops 68287752 | bytes 2382379 | solution.py:125
  255.5 1.8 fusion.52
  257.4 2.5 fusion.54
  267.3 1.8 fusion.52
  269.2 2.5 fusion.54
  279.0 1.8 fusion.52
  280.9 2.5 fusion.54
  290.8 1.8 fusion.52
  292.7 2.5 fusion.54
  302.5 1.8 fusion.52
  304.4 2.5 fusion.54
  314.2 1.8 fusion.52
  316.2 2.5 fusion.54
  326.0 1.8 fusion.52
  327.9 2.5 fusion.54
  337.7 1.8 fusion.52
  339.7 2.5 fusion.54
  343.5 3.7 fusion.25
  347.9 16.4 %fusion.22 = bf16[256,8192]{1,0:T(8,128)(2,1)} fusion(bf16[256,2048]{1,0:T(8,128)(2,1)S(1)} %reshape.99, bf16[1,2048,8192]{2,1,0:T(8,128)(2,1)} %param.15), kind=kOutput, calls=%fused_computation.33 | convolution fusion | flops 8592031744 | bytes 38797312 | tf_op jit(solution)/shard_map/dot_general | solution.py:133
  364.4 48.6 %reduce-scatter.2.cloned.1.call-done = bf16[64,8192]{1,0:T(8,128)(2,1)} async-done(((bf16[256,8192]{1,0:T(8,128)(2,1)}), bf16[64,8192]{1,0:T(8,128)(2,1)}) %reduce-scatter.2.cloned.1.call-update) | async-done | bytes 1048592 | tf_op jit(solution)/shard_map/reduce_scatter | solution.py:132
  (108 shorter events, 31.6 us)
Async XLA Ops:
  31.8 12.7 %all-to-all-start = ((s32[32,1,1]{2,1,0:T(1,128)}), s32[32,1,1]{2,1,0:T(1,128)S(1)}, u32[]{:S(2)}, u32[]{:S(2)}) async-start(s32[32,1,1]{2,1,0:T(1,128)} %copy.31), calls=%async_computation | async-start | bytes 32768 | tf_op jit(solution)/shard_map/all_to_all | solution.py:107
  43.4 10.2 %copy-start.1 = (bf16[1,8,2,256,128]{4,3,2,1,0:T(8,128)(2,1)S(1)}, bf16[1,8,2,256,128]{4,3,2,1,0:T(8,128)(2,1)}, u32[]{:S(2)}) copy-start(bf16[1,8,2,256,128]{4,3,2,1,0:T(8,128)(2,1)} %param.12) | copy-start | bytes 3145732
  44.4 102.6 %copy-start.7 = (s32[32,1,1]{2,1,0:T(1,128)}, s32[32,1,1]{2,1,0:T(1,128)S(1)}, u32[]{:S(2)}) copy-start(s32[32,1,1]{2,1,0:T(1,128)S(1)} %all-to-all-done) | copy-start | bytes 388
  44.4 102.6 %all-to-all-start.1 = ((bf16[32,2,256,128]{3,2,1,0:T(8,128)(2,1)}), bf16[32,2,256,128]{3,2,1,0:T(8,128)(2,1)}, u32[]{:S(2)}, u32[]{:S(2)}) async-start(bf16[32,2,256,128]{3,2,1,0:T(8,128)(2,1)} %gather_fusion.2), calls=%async_computation.1 | async-start | bytes 8388608 | tf_op jit(solution)/shard_map/all_to_all | solution.py:105
  56.7 98.1 %copy-start.2 = (bf16[1,256,2048]{2,1,0:T(8,128)(2,1)S(1)}, bf16[1,256,2048]{2,1,0:T(8,128)(2,1)}, u32[]{:S(2)}) copy-start(bf16[1,256,2048]{2,1,0:T(8,128)(2,1)} %param.10) | copy-start | bytes 3145732
  147.0 101.7 %all-to-all-start.2 = ((bf16[32,2,256,128]{3,2,1,0:T(8,128)(2,1)}), bf16[32,2,256,128]{3,2,1,0:T(8,128)(2,1)}, u32[]{:S(2)}, u32[]{:S(2)}) async-start(bf16[32,2,256,128]{3,2,1,0:T(8,128)(2,1)} %gather_fusion.3), calls=%async_computation.2 | async-start | bytes 8388608 | tf_op jit(solution)/shard_map/all_to_all | solution.py:106
  154.6 0.9 copy-start.5
  154.6 1.0 copy-start.6
  154.6 4.9 %copy-start = (s32[8]{0:T(128)S(1)}, s32[8]{0:T(128)}, u32[]{:S(2)}) copy-start(s32[8]{0:T(128)} %param.17) | copy-start | bytes 100
  154.7 258.3 %reduce-scatter.2.cloned.1.call-start = ((), (), s32[]{:S(2)}) async-start(), calls=%async_computation.4 | async-start | bytes 5242880 | tf_op jit(solution)/shard_map/reduce_scatter | solution.py:132
  156.6 0.8 copy-start.3
  248.8 94.8 %copy-start.4 = (f32[8,2,256,32]{2,3,1,0:T(8,128)S(1)}, f32[8,2,256,32]{2,3,1,0:T(8,128)}, u32[]{:S(2)}) copy-start(f32[8,2,256,32]{2,3,1,0:T(8,128)} %copy-done.3) | copy-start | bytes 1572868
Sparse Core Ops, SparseCore 0:
  364.5 48.3 reduce-scatter.1
where the time goes:
time: 423 us; the launch traced here: 420 us
  waiting for transfers between devices  229 us (54%)
  matrix products  55.2 us (13%)
  local copies, waits for them, and re-layouts  38.5 us (9%)
  loops' own time  34.9 us (8%)
  starting transfers between devices  24.1 us (6%)
  blocking collectives  19.9 us (5%)
  between operations  14.3 us (3%)
    all_to_all x1, waiting for transfers between devices, shards(): lax.all_to_all(send_keys, 'slot', split_axis=0, concat_axis=0, tiled=True)  90.4 us
    all_to_all x1, waiting for transfers between devices, shards(): lax.all_to_all(send_values, 'slot', split_axis=0, concat_axis=0, tiled=True)  89.1 us
    reduce_scatter x1, waiting for transfers between devices, shards(): lax.psum_scatter(jnp.dot(attention, out_weight[0], preferred_element_type...  48.6 us
    another operation x1, loops' own time, shards(): cache_parts = lax.map(attend_node, local_ids)  34.9 us
    dot_general x9, matrix products, partial_softmax(): jnp.einsum('fzo,fol->fzl', softmax_weights.astype(jnp.bfloat16), value_ma...  23.6 us
    unnamed x1, blocking collectives  19.9 us
    dot_general x1, matrix products, shards(): jnp.dot(attention, out_weight[0], preferred_element_type=jnp.float32)  16.4 us
    dot_general x9, matrix products, partial_softmax(): jnp.einsum('syu,swu->syw', query_matrix_rows, key_matrix_rows, preferred_...  15.1 us
  transfers between devices with their start and end apart: 4, of which 4 were waited for; matrix products, arithmetic and copies ran while one was open for 3% of the time, Pallas kernels for 0%

commit v1 on v0

v1 whole, which is shorter than its diff:
```python
import functools

import jax
import jax.numpy as jnp
from jax import lax
from jax.experimental import pallas as pl
from jax.experimental.pallas import tpu as pltpu
from jax.sharding import PartitionSpec as P

BLK = 128
NX = 4
NZ = 8
NTP = 4
NODE = 8
STEP = 32
FAST = 2
CHUNKS = 2

T_SURV = 0
T_FROM = 8
T_RANK = 16
T_LEN = 24
T_REL = 32
T_SEL = 40
T_SIZE = 64


def zperm(d):
    return [(s, (s + NX * d) % (NX * NZ)) for s in range(NX * NZ)]


def xperm(d):
    return [(s, (s // NX) * NX + (s % NX + d) % NX) for s in range(NX * NZ)]


def yperm(d):
    return [(t, (t + d) % NTP) for t in range(NTP)]


def plan_body(here_ref, parents_ref, blocks_ref, plan_ref):
    here = here_ref[0]
    row = here // NX
    col = here % NX
    for i in range(T_SIZE):
        plan_ref[i] = 0

    def surv_step(j, count):
        keep = parents_ref[here * NODE + j] == here * NODE + j

        @pl.when(keep)
        def _():
            plan_ref[T_SURV + jnp.minimum(count, 1)] = j

        return count + keep.astype(jnp.int32)

    lax.fori_loop(0, NODE, surv_step, jnp.int32(0))

    def own_step(j, counts):
        slot = here * NODE + j
        parent = parents_ref[slot]
        moving = parent != slot
        dist = (col - (parent // NODE) % NX + NX) % NX
        plan_ref[T_LEN + j] = blocks_ref[parent] * BLK
        plan_ref[T_FROM + j] = jnp.where(moving, dist, NX)
        rank = jnp.int32(0)
        out = []
        for d in range(NX):
            hit = moving & (dist == d)
            rank = jnp.where(hit, counts[d], rank)
            out.append(counts[d] + hit.astype(jnp.int32))
        plan_ref[T_RANK + j] = jnp.minimum(rank, FAST - 1)
        return tuple(out)

    lax.fori_loop(0, NODE, own_step, (jnp.int32(0),) * NX)

    for d in range(NX):
        peer = row * NX + (col + d) % NX

        def peer_step(j, count, peer=peer, d=d):
            slot = peer * NODE + j
            parent = parents_ref[slot]
            source = parent // NODE
            hit = (parent != slot) & (source % NX == col)

            @pl.when(hit & (count < FAST))
            def _():
                def below(k, seen):
                    node = source * NODE + k
                    is_below = (node < parent) & (parents_ref[node] == node)
                    return seen | is_below.astype(jnp.int32)

                order = lax.fori_loop(0, NODE, below, jnp.int32(0))
                plan_ref[T_REL + d * FAST + count] = (row - source // NX + NZ) % NZ
                plan_ref[T_SEL + d * FAST + count] = order

            return count + hit.astype(jnp.int32)

        lax.fori_loop(0, NODE, peer_step, jnp.int32(0))


def make_plan(here, parents, blocks):
    smem = pl.BlockSpec(memory_space=pltpu.SMEM)
    return pl.pallas_call(
        plan_body,
        out_shape=jax.ShapeDtypeStruct((T_SIZE,), jnp.int32),
        in_specs=[smem, smem, smem],
        out_specs=smem,
        name="plan",
    )(here, parents, blocks)


def pack_body(plan_ref, keys_ref, values_ref, first_ref, second_ref, sems):
    copies = []
    for s in range(2):
        node = plan_ref[T_SURV + s]
        for b, out in enumerate((first_ref, second_ref)):
            for kv, src in enumerate((keys_ref, values_ref)):
                copies.append(
                    pltpu.make_async_copy(
                        src.at[node, :, pl.ds(b * BLK, BLK), :],
                        out.at[kv, s],
                        sems.at[len(copies)],
                    )
                )
    for c in copies:
        c.start()
    for c in copies:
        c.wait()


def pack(plan, keys, values):
    heads, _, dim = keys.shape[1:]
    shape = jax.ShapeDtypeStruct((2, 2, heads, BLK, dim), keys.dtype)
    hbm = pl.BlockSpec(memory_space=pl.ANY)
    return pl.pallas_call(
        pack_body,
        out_shape=(shape, shape),
        in_specs=[pl.BlockSpec(memory_space=pltpu.SMEM), hbm, hbm],
        out_specs=(hbm, hbm),
        scratch_shapes=[pltpu.SemaphoreType.DMA((8,))],
        name="pack",
    )(plan, keys, values)


def ring_gather(own):
    up, down = own, own
    got = {0: (own, own)}
    for k in (1, 2, 3):
        up = lax.ppermute(up, "slot", zperm(1))
        down = lax.ppermute(down, "slot", zperm(-1))
        got[k] = (up, up)
        got[NZ - k] = (down, down)
    half_up = lax.ppermute(up[0:1], "slot", zperm(1))
    half_down = lax.ppermute(down[1:2], "slot", zperm(-1))
    got[4] = (half_up, half_down)
    return got


def select_body(plan_ref, *refs):
    srcs = refs[:9]
    outs = refs[9 : 9 + NX]
    sems = refs[9 + NX]

    def source(rel, kv):
        if rel < 4:
            return srcs[rel], kv
        if rel == 4:
            return srcs[4 + kv], 0
        return srcs[rel + 1], kv

    def issue(start):
        for d in range(NX):
            for i in range(FAST):
                rel = plan_ref[T_REL + d * FAST + i]
                order = plan_ref[T_SEL + d * FAST + i]
                for kv in range(2):
                    sem = sems.at[(d * FAST + i) * 2 + kv]
                    if start:
                        for r in range(NZ):
                            ref, lead = source(r, kv)

                            @pl.when(rel == r)
                            def _(ref=ref, lead=lead):
                                pltpu.make_async_copy(
                                    ref.at[lead, order], outs[d].at[kv, i], sem
                                ).start()
                    else:
                        pltpu.make_async_copy(srcs[0].at[kv, 0], outs[d].at[kv, i], sem).wait()

    issue(True)
    issue(False)


def select(plan, got):
    own = got[0][0]
    srcs = [got[r][0] for r in range(4)] + [got[4][0], got[4][1]] + [got[r][0] for r in (5, 6, 7)]
    shape = jax.ShapeDtypeStruct((2, FAST) + own.shape[2:], own.dtype)
    hbm = pl.BlockSpec(memory_space=pl.ANY)
    return pl.pallas_call(
        select_body,
        out_shape=(shape,) * NX,
        in_specs=[pl.BlockSpec(memory_space=pltpu.SMEM)] + [hbm] * 9,
        out_specs=(hbm,) * NX,
        scratch_shapes=[pltpu.SemaphoreType.DMA((NX * FAST * 2,))],
        name="select",
    )(plan, *srcs)


def place_body(plan_ref, *refs):
    caches = refs[0:2]
    firsts = refs[2 : 2 + NX]
    seconds = refs[2 + NX : 2 + 2 * NX]
    outs = refs[2 + 2 * NX : 4 + 2 * NX]
    sems = refs[4 + 2 * NX]

    for j in range(NODE):
        dist = plan_ref[T_FROM + j]
        rank = plan_ref[T_RANK + j]
        for kv in range(2):
            for b in range(2):
                dst = outs[kv].at[j, :, pl.ds(b * BLK, BLK), :]
                sem = sems.at[(j * 2 + kv) * 2 + b]

                @pl.when(dist == NX)
                def _(kv=kv, b=b, dst=dst, sem=sem, j=j):
                    pltpu.make_async_copy(
                        caches[kv].at[j, :, pl.ds(b * BLK, BLK), :], dst, sem
                    ).start()

                for d in range(NX):

                    @pl.when(dist == d)
                    def _(kv=kv, b=b, dst=dst, sem=sem, rank=rank, d=d):
                        src = (firsts, seconds)[b][d]
                        pltpu.make_async_copy(src.at[kv, rank], dst, sem).start()

    for j in range(NODE):
        for kv in range(2):
            for b in range(2):
                pltpu.make_async_copy(
                    caches[kv].at[j, :, pl.ds(b * BLK, BLK), :],
                    outs[kv].at[j, :, pl.ds(b * BLK, BLK), :],
                    sems.at[(j * 2 + kv) * 2 + b],
                ).wait()


def place(plan, keys, values, firsts, seconds):
    hbm = pl.BlockSpec(memory_space=pl.ANY)
    shape = jax.ShapeDtypeStruct(keys.shape, keys.dtype)
    return pl.pallas_call(
        place_body,
        out_shape=(shape, shape),
        in_specs=[pl.BlockSpec(memory_space=pltpu.SMEM)] + [hbm] * (2 + 2 * NX),
        out_specs=(hbm, hbm),
        scratch_shapes=[pltpu.SemaphoreType.DMA((NODE * 4,))],
        name="place",
    )(plan, keys, values, *firsts, *seconds)


def attend_body(heads, group, dim, scale, plan_ref, q_ref, k_ref, v_ref, nk_ref, nv_ref, out_ref):
    length = plan_ref[T_LEN + pl.program_id(0)]
    rows = STEP * group
    tokens = k_ref.shape[2]
    nt = (((1,), (1,)), ((), ()))
    nn = (((1,), (0,)), ((), ()))
    cache_ok = lax.broadcasted_iota(jnp.int32, (rows, tokens), 1) < length
    step_of = lax.broadcasted_iota(jnp.int32, (rows, STEP), 0) % STEP
    step_ok = lax.broadcasted_iota(jnp.int32, (rows, STEP), 1) <= step_of
    for h in range(heads):
        base = h * group * dim
        q = jnp.concatenate(
            [q_ref[:, base + g * dim : base + (g + 1) * dim] for g in range(group)], axis=0
        )
        nk = nk_ref[:, h * dim : (h + 1) * dim]
        nv = nv_ref[:, h * dim : (h + 1) * dim]
        sc = lax.dot_general(q, k_ref[0, h], nt, preferred_element_type=jnp.float32) * scale
        ss = lax.dot_general(q, nk, nt, preferred_element_type=jnp.float32) * scale
        sc = jnp.where(cache_ok, sc, -jnp.inf)
        ss = jnp.where(step_ok, ss, -jnp.inf)
        top = jnp.maximum(
            jnp.max(sc, axis=1, keepdims=True), jnp.max(ss, axis=1, keepdims=True)
        )
        pc = jnp.exp(sc - top)
        ps = jnp.exp(ss - top)
        total = jnp.sum(pc, axis=1, keepdims=True) + jnp.sum(ps, axis=1, keepdims=True)
        o = lax.dot_general(
            pc.astype(jnp.bfloat16), v_ref[0, h], nn, preferred_element_type=jnp.float32
        ) + lax.dot_general(ps.astype(jnp.bfloat16), nv, nn, preferred_element_type=jnp.float32)
        o = (o / total).astype(out_ref.dtype)
        for g in range(group):
            out_ref[:, base + g * dim : base + (g + 1) * dim] = o[g * STEP : (g + 1) * STEP]


def attend(plan, queries, keys, values, new_keys, new_values):
    heads, tokens, dim = keys.shape[1:]
    width = queries.shape[1]
    group = width // (heads * dim)
    kv_spec = pl.BlockSpec((1, heads, tokens, dim), lambda n, p: (n, 0, 0, 0))
    q_spec = pl.BlockSpec((STEP, width), lambda n, p: (n, 0))
    n_spec = pl.BlockSpec((STEP, heads * dim), lambda n, p: (n, 0))
    return pl.pallas_call(
        functools.partial(attend_body, heads, group, dim, float(dim) ** -0.5),
        out_shape=jax.ShapeDtypeStruct(queries.shape, queries.dtype),
        grid_spec=pltpu.PrefetchScalarGridSpec(
            num_scalar_prefetch=1,
            grid=(NODE,),
            in_specs=[q_spec, kv_spec, kv_spec, n_spec, n_spec],
            out_specs=q_spec,
        ),
        name="attend",
    )(plan, queries, keys, values, new_keys, new_values)


def project_body(tp_ref, att_ref, w_ref, r0_ref, r1_ref, r2_ref, r3_ref, rel_ref):
    part = att_ref.shape[0] // NTP

    @pl.when(pl.program_id(0) == 0)
    def _():
        for d in range(NTP):
            row = pl.multiple_of(((tp_ref[0] + d) % NTP) * part, part)
            rel_ref[d * part : (d + 1) * part, :] = att_ref[pl.ds(row, part), :]

    res = jnp.dot(rel_ref[...], w_ref[...], preferred_element_type=jnp.float32)
    for d, ref in enumerate((r0_ref, r1_ref, r2_ref, r3_ref)):
        ref[...] = res[d * part : (d + 1) * part].astype(ref.dtype)


def project(tp, att, weight, chunk, tile):
    rows, inner = att.shape
    width = weight.shape[1] // CHUNKS
    steps = width // tile
    part = rows // NTP
    out = jax.ShapeDtypeStruct((part, width), att.dtype)
    out_spec = pl.BlockSpec((part, tile), lambda n, t: (0, n))
    return pl.pallas_call(
        project_body,
        out_shape=(out,) * NTP,
        grid_spec=pltpu.PrefetchScalarGridSpec(
            num_scalar_prefetch=1,
            grid=(steps,),
            in_specs=[
                pl.BlockSpec((rows, inner), lambda n, t: (0, 0)),
                pl.BlockSpec((inner, tile), lambda n, t: (0, chunk * steps + n)),
            ],
            out_specs=(out_spec,) * NTP,
            scratch_shapes=[pltpu.VMEM((rows, inner), att.dtype)],
        ),
        name="project",
    )(tp, att, weight)


def add2(a, b):
    return (a.astype(jnp.float32) + b.astype(jnp.float32)).astype(a.dtype)


def scatter_sum(parts):
    r0, r1, r2, r3 = parts
    half = r0.shape[1] // 2
    up, down = yperm(1), yperm(-1)
    relay_a = lax.ppermute(r2[:, :half], "tp", up)
    relay_b = lax.ppermute(r2[:, half:], "tp", down)
    direct_b = lax.ppermute(r1[:, half:], "tp", up)
    direct_a = lax.ppermute(r3[:, :half], "tp", down)
    far_a = lax.ppermute(add2(r1[:, :half], relay_a), "tp", up)
    far_b = lax.ppermute(add2(r3[:, half:], relay_b), "tp", down)
    f32 = jnp.float32
    out_a = r0[:, :half].astype(f32) + far_a.astype(f32) + direct_a.astype(f32)
    out_b = r0[:, half:].astype(f32) + far_b.astype(f32) + direct_b.astype(f32)
    return [out_a.astype(r0.dtype), out_b.astype(r0.dtype)]


def general_fetch(parents, keys, values):
    slot_count = lax.axis_size("slot")
    slot_here = lax.axis_index("slot")
    moving_all = parents != jnp.arange(parents.shape[0], dtype=jnp.int32)
    from_here = (moving_all & (parents // NODE == slot_here)).reshape(slot_count, NODE)
    local = (parents % NODE).reshape(slot_count, NODE)
    send_node = jnp.sum(jnp.where(from_here, local, 0), axis=1)
    got_keys = lax.all_to_all(keys[send_node], "slot", 0, 0, tiled=True)
    got_values = lax.all_to_all(values[send_node], "slot", 0, 0, tiled=True)
    own = lax.dynamic_slice_in_dim(parents, slot_here * NODE, NODE)
    moving = (own != slot_here * NODE + jnp.arange(NODE, dtype=jnp.int32))[:, None, None, None]
    source = own // NODE
    return (
        jnp.where(moving, got_keys[source], keys),
        jnp.where(moving, got_values[source], values),
    )


def shards(
    queries, cache_keys, cache_values, new_keys, new_values, out_weight, fork_src, cache_blocks
):
    keys, values = cache_keys[0], cache_values[0]
    slot_here = lax.axis_index("slot").astype(jnp.int32)
    tp_here = lax.axis_index("tp").astype(jnp.int32).reshape(1)
    peers = lax.axis_size("role") * lax.axis_size("slot")
    meta = jnp.concatenate([fork_src, cache_blocks])
    meta = jnp.broadcast_to(meta[None], (peers, meta.shape[0]))
    meta = lax.all_to_all(meta, ("role", "slot"), 0, 0, tiled=True)
    n_src = fork_src.shape[0]
    parents = meta[:, :n_src].reshape(-1)
    blocks = meta[: peers // 2, n_src:].reshape(-1)
    plan = make_plan(slot_here.reshape(1), parents, blocks)

    slots = jnp.arange(parents.shape[0], dtype=jnp.int32)
    column = jnp.where(parents != slots, (parents // NODE) % NX, NX).reshape(-1, NODE)
    load = jnp.stack([jnp.sum((column == c).astype(jnp.int32), axis=1) for c in range(NX)])
    fits = jnp.max(load) <= FAST

    first, second = pack(plan, keys, values)
    got_first = ring_gather(first)
    got_second = ring_gather(second)

    def fast(_):
        moved = []
        for got in (got_first, got_second):
            outs = select(plan, got)
            moved.append([outs[0]] + [lax.ppermute(outs[d], "slot", xperm(d)) for d in (1, 2, 3)])
        return place(plan, keys, values, moved[0], moved[1])

    def general(_):
        return general_fetch(parents, keys, values)

    node_keys, node_values = lax.cond(fits, fast, general, 0)
    att = attend(plan, queries[0], node_keys, node_values, new_keys[0], new_values[0])
    pieces = []
    for c in range(CHUNKS):
        pieces += scatter_sum(project(tp_here, att, out_weight[0], c, 1024))
    return jnp.concatenate(pieces, axis=1)[None]


def solution(mesh):
    in_specs = (
        P("role", "slot", "tp"),
        P("role", "slot", "tp", None, None),
        P("role", "slot", "tp", None, None),
        P("role", "slot", "tp"),
        P("role", "slot", "tp"),
        P("role", "tp", None),
        P(("role", "slot")),
        P("slot"),
    )
    out_specs = P("role", ("slot", "tp"), None)
    return jax.shard_map(shards, mesh=mesh, in_specs=in_specs, out_specs=out_specs, check_vma=False)
```

time: 423 us -> 247 us (0.58); the launches traced: 420 us -> 250 us
  waiting for transfers between devices: 229 us -> 54.3 us
  Pallas kernels: 0 us -> 112 us
  matrix products: 55.2 us -> 0 us
  starting transfers between devices: 24.1 us -> 66.5 us
  loops' own time: 34.9 us -> 0.31 us
  local copies, waits for them, and re-layouts: 38.5 us -> 7.84 us
  blocking collectives: 19.9 us -> 0 us
  between operations: 14.3 us -> 2.79 us
    all_to_all x3 -> x1, waiting for transfers between devices: 180 us -> 5.16 us  [shards(): meta = lax.all_to_all(meta, ('role', 'slot'), 0, 0, tiled=True)]
    pallas_call x0 -> x8, Pallas kernels: none -> 112 us  [the longest x2 51.3 us: select(): pl.pallas_call(select_body, out_shape=(shape,) * NX, in_specs=[pl.BlockSp...]
    ppermute x0 -> x34, starting transfers between devices: none -> 55.9 us  [the longest x6 16.2 us: ring_gather(): up = lax.ppermute(up, 'slot', zperm(1))]
    dot_general x19 -> x0, matrix products: 55.2 us -> none  [the longest x9 23.6 us: partial_softmax(): jnp.einsum('fzo,fol->fzl', softmax_weights.astype(jnp.bfloat16), value_ma...]
    ppermute x0 -> x34, waiting for transfers between devices: none -> 49.2 us  [the longest x6 14.6 us: ring_gather(): down = lax.ppermute(down, 'slot', zperm(-1))]
    reduce_scatter x1 -> x0, waiting for transfers between devices: 48.6 us -> none  [shards(): lax.psum_scatter(jnp.dot(attention, out_weight[0], preferred_element_type...]
    another operation x1, loops' own time: 34.9 us -> 0.31 us  [shards(): node_keys, node_values = lax.cond(fits, fast, general, 0)]
    unnamed x1 -> x0, blocking collectives: 19.9 us -> none
  transfers between devices with their start and end apart: 4 -> 35, of which waited for: 4 -> 18; matrix products, arithmetic and copies ran while one was open for 3% -> 3% of each run, Pallas kernels for 0% -> 10%
where the time goes in v1:
time: 247 us; the launch traced here: 250 us
  Pallas kernels  112 us (45%)
  starting transfers between devices  66.5 us (27%)
  waiting for transfers between devices  54.3 us (22%)
  local copies, waits for them, and re-layouts  7.84 us (3%)
  other arithmetic  5.78 us (2%)
  between operations  2.79 us (1%)
    pallas_call x2, Pallas kernels, select(): pl.pallas_call(select_body, out_shape=(shape,) * NX, in_specs=[pl.BlockSp...  51.3 us
    pallas_call x1, Pallas kernels, place(): pl.pallas_call(place_body, out_shape=(shape, shape), in_specs=[pl.BlockSp...  25.9 us
    pallas_call x2, Pallas kernels, project(): pl.pallas_call(project_body, out_shape=(out,) * NTP, grid_spec=pltpu.Pref...  21.1 us
    ppermute x6, starting transfers between devices, ring_gather(): up = lax.ppermute(up, 'slot', zperm(1))  16.2 us
    ppermute x6, waiting for transfers between devices, ring_gather(): down = lax.ppermute(down, 'slot', zperm(-1))  14.6 us
    ppermute x6, starting transfers between devices, fast(): lax.ppermute(outs[d], 'slot', xperm(d))  13.7 us
    ppermute x6, waiting for transfers between devices, fast(): lax.ppermute(outs[d], 'slot', xperm(d))  10.9 us
    all_to_all x1, starting transfers between devices, shards(): meta = lax.all_to_all(meta, ('role', 'slot'), 0, 0, tiled=True)  10.6 us
  transfers between devices with their start and end apart: 35, of which 18 were waited for; matrix products, arithmetic and copies ran while one was open for 3% of the time, Pallas kernels for 10%

profile of v1, /device:TPU:102, one launch (start us, length us, event | category | flops | bytes accessed | tf_op | source)
XLA Modules:
  0.0 250.0 jit_solution(17718129413788365480)
XLA Ops:
  1.4 10.6 %all-to-all-start.2 = ((s32[64,1,12]{2,1,0:T(1,128)}), s32[64,1,12]{2,1,0:T(1,128)S(1)}, u32[]{:S(2)}, u32[]{:S(2)}) async-start(s32[64,1,12]{2,1,0:T(1,128)} %broadcast_in_dim.31), calls=%async_computation.2 | async-start | bytes 65536 | tf_op jit(solution)/shard_map/all_to_all | solution.py:399
  12.0 5.2 %all-to-all-done.2 = s32[64,1,12]{2,1,0:T(1,128)S(1)} async-done(((s32[64,1,12]{2,1,0:T(1,128)}), s32[64,1,12]{2,1,0:T(1,128)S(1)}, u32[]{:S(2)}, u32[]{:S(2)}) %all-to-all-start.2) | async-done | bytes 3104 | tf_op jit(solution)/shard_map/all_to_all | solution.py:399
  18.0 3.1 %plan.1.plan_ref = s32[64]{0:T(128)S(1)} custom-call(s32[1]{0:T(128)} %bitcast.3.here_ref, s32[256]{0:T(256)S(1)} %reshape.53.parents_ref, s32[256]{0:T(256)} %reshape.54.blocks_ref), custom_call_target="tpu_custom_call" | custom-call | tf_op jit(solution)/shard_map/plan/pallas_call | solution.py:103
  26.5 2.9 %collective-permute-start.14 = (bf16[2,2,2,128,128]{4,3,2,1,0:T(8,128)(2,1)S(1)}, bf16[2,2,2,128,128]{4,3,2,1,0:T(8,128)(2,1)}, u32[]{:S(2)}, u32[]{:S(2)}) collective-permute-start(bf16[2,2,2,128,128]{4,3,2,1,0:T(8,128)(2,1)S(1)} %get-tuple-element.98), channel_id=1, source_target_pairs={{0,16},{4,20},{8,24},{12,28},{16,32},{20,36},{24,40},{28,44},{32,4... | collective-permute-start | bytes 786440 | tf_op jit(solution)/shard_map/ppermute | solution.py:149
  29.4 3.9 %collective-permute-done.10 = bf16[2,2,2,128,128]{4,3,2,1,0:T(8,128)(2,1)S(1)} collective-permute-done((bf16[2,2,2,128,128]{4,3,2,1,0:T(8,128)(2,1)S(1)}, bf16[2,2,2,128,128]{4,3,2,1,0:T(8,128)(2,1)S(1)}, u32[]{:S(2)}, u32[]{:S(2)}) %collective-permute-start.10) | collective-permute-done | bytes 262176 | tf_op jit(solution)/shard_map/ppermute | solution.py:150
  33.6 2.9 %collective-permute-start.7 = (bf16[2,2,2,128,128]{4,3,2,1,0:T(8,128)(2,1)S(1)}, bf16[2,2,2,128,128]{4,3,2,1,0:T(8,128)(2,1)}, u32[]{:S(2)}, u32[]{:S(2)}) collective-permute-start(bf16[2,2,2,128,128]{4,3,2,1,0:T(8,128)(2,1)S(1)} %collective-permute-done.6), channel_id=1, source_target_pairs={{0,16},{4,20},{8,24},{12,28},{16,32},{20,36},{24,40},{28,44},{32,4... | collective-permute-start | bytes 786440 | tf_op jit(solution)/shard_map/ppermute | solution.py:149
  39.4 2.9 %collective-permute-start.15 = (bf16[2,2,2,128,128]{4,3,2,1,0:T(8,128)(2,1)}, bf16[2,2,2,128,128]{4,3,2,1,0:T(8,128)(2,1)}, u32[]{:S(2)}, u32[]{:S(2)}) collective-permute-start(bf16[2,2,2,128,128]{4,3,2,1,0:T(8,128)(2,1)} %collective-permute-done.14), channel_id=1, source_target_pairs={{0,16},{4,20},{8,24},{12,28},{16,32},{20,36},{24,40},{28,44},{32,4... | collective-permute-start | bytes 786440 | tf_op jit(solution)/shard_map/ppermute | solution.py:149
  42.3 2.4 collective-permute-done.11
  45.0 2.9 %collective-permute-start.8 = (bf16[2,2,2,128,128]{4,3,2,1,0:T(8,128)(2,1)}, bf16[2,2,2,128,128]{4,3,2,1,0:T(8,128)(2,1)S(1)}, u32[]{:S(2)}, u32[]{:S(2)}) collective-permute-start(bf16[2,2,2,128,128]{4,3,2,1,0:T(8,128)(2,1)} %collective-permute-done.7), channel_id=1, source_target_pairs={{0,16},{4,20},{8,24},{12,28},{16,32},{20,36},{24,40},{28,44},{32,4... | collective-permute-start | bytes 786440 | tf_op jit(solution)/shard_map/ppermute | solution.py:149
  47.9 2.4 collective-permute-done.19
  50.6 2.9 %collective-permute-start.16 = (bf16[2,2,2,128,128]{4,3,2,1,0:T(8,128)(2,1)}, bf16[2,2,2,128,128]{4,3,2,1,0:T(8,128)(2,1)S(1)}, u32[]{:S(2)}, u32[]{:S(2)}) collective-permute-start(bf16[2,2,2,128,128]{4,3,2,1,0:T(8,128)(2,1)} %collective-permute-done.15), channel_id=1, source_target_pairs={{0,16},{4,20},{8,24},{12,28},{16,32},{20,36},{24,40},{28,44},{32,4... | collective-permute-start | bytes 786440 | tf_op jit(solution)/shard_map/ppermute | solution.py:149
  56.9 3.2 %collective-permute-start.9 = (bf16[1,2,2,128,128]{4,3,2,1,0:T(8,128)(2,1)S(1)}, bf16[1,2,2,128,128]{4,3,2,1,0:T(8,128)(2,1)}, u32[]{:S(2)}, u32[]{:S(2)}) collective-permute-start(bf16[1,2,2,128,128]{4,3,2,1,0:T(8,128)(2,1)S(1)} %slice.98), channel_id=1, source_target_pairs={{0,16},{4,20},{8,24},{12,28},{16,32},{20,36},{24,40},{28,44},{32,4... | collective-permute-start | bytes 393224 | tf_op jit(solution)/shard_map/ppermute | solution.py:153
  63.2 3.0 %collective-permute-start.17 = (bf16[1,2,2,128,128]{4,3,2,1,0:T(8,128)(2,1)S(1)}, bf16[1,2,2,128,128]{4,3,2,1,0:T(8,128)(2,1)}, u32[]{:S(2)}, u32[]{:S(2)}) collective-permute-start(bf16[1,2,2,128,128]{4,3,2,1,0:T(8,128)(2,1)S(1)} %slice.100), channel_id=1, source_target_pairs={{0,16},{4,20},{8,24},{12,28},{16,32},{20,36},{24,40},{28,44},{32,4... | collective-permute-start | bytes 393224 | tf_op jit(solution)/shard_map/ppermute | solution.py:153
  72.4 102.9 %conditional.1 = ((bf16[8,2,256,128]{3,2,1,0:T(8,128)(2,1)}, bf16[8,2,256,128]{3,2,1,0:T(8,128)(2,1)S(1)})) conditional(s32[]{:T(128)} %convert_element_type.107, (s32[256]{0:T(256)S(1)}, bf16[8,2,256,128]{3,2,1,0:T(8,128)(2,1)}, bf16[8,2,256,128]{3,2,1,0:T(8,128)(2,1)}) %tuple.29, (s32[64]{0:T(128)S(1)}, ...), branch_computations={%region_12.14_spmd, %region_14.15_spmd} | conditional | flops 1056999 | bytes 60831936 | solution.py:424
  72.4 25.6 %select.38 = (bf16[2,2,2,128,128]{4,3,2,1,0:T(8,128)(2,1)}, bf16[2,2,2,128,128]{4,3,2,1,0:T(8,128)(2,1)}, bf16[2,2,2,128,128]{4,3,2,1,0:T(8,128)(2,1)}, bf16[2,2,2,128,128]{4,3,2,1,0:T(8,128)(2,1)}) custom-call(s32[64]{0:T(128)S(1)} %get-tuple-element.56.plan_ref, bf16[2,2,2,128,128]{4,3,2,1,0:T(8,128)(2,1)S(1)} %get-tuple-element.59.refs_0_, ...), custom_call_target="tpu_custom_call" | custom-call | tf_op jit(solution)/shard_map/cond/branch_1_fun/select/pallas_call | solution.py:199
  100.2 25.6 %select.39 = (bf16[2,2,2,128,128]{4,3,2,1,0:T(8,128)(2,1)}, bf16[2,2,2,128,128]{4,3,2,1,0:T(8,128)(2,1)}, bf16[2,2,2,128,128]{4,3,2,1,0:T(8,128)(2,1)}, bf16[2,2,2,128,128]{4,3,2,1,0:T(8,128)(2,1)}) custom-call(s32[64]{0:T(128)S(1)} %get-tuple-element.56.plan_ref, bf16[2,2,2,128,128]{4,3,2,1,0:T(8,128)(2,1)S(1)} %get-tuple-element.72.refs_0_, ...), custom_call_target="tpu_custom_call" | custom-call | tf_op jit(solution)/shard_map/cond/branch_1_fun/select/pallas_call | solution.py:199
  125.8 10.7 %collective-permute-start.3 = (bf16[2,2,2,128,128]{4,3,2,1,0:T(8,128)(2,1)}, bf16[2,2,2,128,128]{4,3,2,1,0:T(8,128)(2,1)S(1)}, u32[]{:S(2)}, u32[]{:S(2)}) collective-permute-start(bf16[2,2,2,128,128]{4,3,2,1,0:T(8,128)(2,1)} %get-tuple-element.82), channel_id=1, source_target_pairs={{0,4},{4,8},{8,12},{12,0},{16,20},{20,24},{24,28},{28,16},{32,36},... | collective-permute-start | bytes 786440 | tf_op jit(solution)/shard_map/cond/branch_1_fun/ppermute | solution.py:418
  137.5 7.6 %collective-permute-done.3.refs_7_ = bf16[2,2,2,128,128]{4,3,2,1,0:T(8,128)(2,1)S(1)} collective-permute-done((bf16[2,2,2,128,128]{4,3,2,1,0:T(8,128)(2,1)}, bf16[2,2,2,128,128]{4,3,2,1,0:T(8,128)(2,1)S(1)}, u32[]{:S(2)}, u32[]{:S(2)}) %collective-permute-start.3) | collective-permute-done | bytes 262176 | tf_op jit(solution)/shard_map/cond/branch_1_fun/ppermute | solution.py:418
  146.0 2.5 collective-permute-done.5.refs_9_
  149.1 25.9 %place.1 = (bf16[8,2,256,128]{3,2,1,0:T(8,128)(2,1)}, bf16[8,2,256,128]{3,2,1,0:T(8,128)(2,1)S(1)}) custom-call(s32[64]{0:T(128)S(1)} %get-tuple-element.56.plan_ref, bf16[8,2,256,128]{3,2,1,0:T(8,128)(2,1)S(1)} %copy-done.1, bf16[8,2,256,128]{3,2,1,0:T(8,128)(2,1)S(1)} %copy-done.3, bf16[2,2,2,128,128]{4,3,2,1,0:T(8,128)(2,1)} %get-tuple-element.68.refs_2_, ...), custom_call_target="tpu_custom_call" | custom-call | tf_op jit(solution)/shard_map/cond/branch_1_fun/place/pallas_call | solution.py:250
  175.2 9.4 %attend.1.att_ref = bf16[256,2048]{1,0:T(8,128)(2,1)} custom-call(s32[64]{0:T(128)S(1)} %plan.1.plan_ref, bf16[256,2048]{1,0:T(8,128)(2,1)} %bitcast.23, bf16[8,2,256,128]{3,2,1,0:T(8,128)(2,1)} %get-tuple-element.99.k_ref, bf16[8,2,256,128]{3,2,1,0:T(8,128)(2,1)S(1)} %get-tuple-element.100.v_ref, bf16[256,256]{1,0:T(8,128)(2,1)} %bitcast.26, ...), custom_call_target="tpu_custom_call" | custom-call | tf_op jit(solution)/shard_map/attend/pallas_call | solution.py:301
  184.6 9.9 %project.3 = (bf16[64,4096]{1,0:T(8,128)(2,1)}, bf16[64,4096]{1,0:T(8,128)(2,1)}, bf16[64,4096]{1,0:T(8,128)(2,1)}, bf16[64,4096]{1,0:T(8,128)(2,1)}) custom-call(s32[1]{0:T(128)} %bitcast.2.tp_ref, bf16[256,2048]{1,0:T(8,128)(2,1)} %attend.1.att_ref, bf16[2048,8192]{1,0:T(8,128)(2,1)} %bitcast.15), custom_call_target="tpu_custom_call" | custom-call | tf_op jit(solution)/shard_map/project/pallas_call | solution.py:335
  194.5 11.2 %project.2 = (bf16[64,4096]{1,0:T(8,128)(2,1)}, bf16[64,4096]{1,0:T(8,128)(2,1)}, bf16[64,4096]{1,0:T(8,128)(2,1)}, bf16[64,4096]{1,0:T(8,128)(2,1)}) custom-call(s32[1]{0:T(128)} %bitcast.2.tp_ref, bf16[256,2048]{1,0:T(8,128)(2,1)} %attend.1.att_ref, bf16[2048,8192]{1,0:T(8,128)(2,1)} %bitcast.16), custom_call_target="tpu_custom_call" | custom-call | tf_op jit(solution)/shard_map/project/pallas_call | solution.py:335
  205.9 3.1 %collective-permute-start.30 = (bf16[64,2048]{1,0:T(8,128)(2,1)S(1)}, bf16[64,2048]{1,0:T(8,128)(2,1)S(1)}, u32[]{:S(2)}, u32[]{:S(2)}) collective-permute-start(bf16[64,2048]{1,0:T(8,128)(2,1)S(1)} %slice.83), channel_id=1, source_target_pairs={{0,3},{1,0},{2,1},{3,2},{4,7},{5,4},{6,5},{7,6},{8,11},{9,8},{10,9... | collective-permute-start | bytes 786440 | tf_op jit(solution)/shard_map/ppermute | solution.py:363
  209.7 2.7 %collective-permute-start.31 = (bf16[64,2048]{1,0:T(8,128)(2,1)S(1)}, bf16[64,2048]{1,0:T(8,128)(2,1)S(1)}, u32[]{:S(2)}, u32[]{:S(2)}) collective-permute-start(bf16[64,2048]{1,0:T(8,128)(2,1)S(1)} %get-tuple-element.122), channel_id=1, source_target_pairs={{0,3},{1,0},{2,1},{3,2},{4,7},{5,4},{6,5},{7,6},{8,11},{9,8},{10,9... | collective-permute-start | bytes 786440 | tf_op jit(solution)/shard_map/ppermute | solution.py:361
  217.4 4.8 %collective-permute-done.28 = bf16[64,2048]{1,0:T(8,128)(2,1)S(1)} collective-permute-done((bf16[64,2048]{1,0:T(8,128)(2,1)S(1)}, bf16[64,2048]{1,0:T(8,128)(2,1)S(1)}, u32[]{:S(2)}, u32[]{:S(2)}) %collective-permute-start.28) | collective-permute-done | bytes 262176 | tf_op jit(solution)/shard_map/ppermute | solution.py:360
  222.3 3.3 %collective-permute-start.25 = (bf16[64,2048]{1,0:T(8,128)(2,1)S(1)}, bf16[64,2048]{1,0:T(8,128)(2,1)S(1)}, u32[]{:S(2)}, u32[]{:S(2)}) collective-permute-start(bf16[64,2048]{1,0:T(8,128)(2,1)S(1)} %get-tuple-element.118), channel_id=1, source_target_pairs={{0,3},{1,0},{2,1},{3,2},{4,7},{5,4},{6,5},{7,6},{8,11},{9,8},{10,9... | collective-permute-start | bytes 786440 | tf_op jit(solution)/shard_map/ppermute | solution.py:361
  225.7 4.1 %collective-permute-done.22 = bf16[64,2048]{1,0:T(8,128)(2,1)S(1)} collective-permute-done((bf16[64,2048]{1,0:T(8,128)(2,1)S(1)}, bf16[64,2048]{1,0:T(8,128)(2,1)S(1)}, u32[]{:S(2)}, u32[]{:S(2)}) %collective-permute-start.22) | collective-permute-done | bytes 262176 | tf_op jit(solution)/shard_map/ppermute | solution.py:360
  230.1 3.7 %collective-permute-start.32 = (bf16[64,2048]{1,0:T(8,128)(2,1)S(1)}, bf16[64,2048]{1,0:T(8,128)(2,1)S(1)}, u32[]{:S(2)}, u32[]{:S(2)}) collective-permute-start(bf16[64,2048]{1,0:T(8,128)(2,1)S(1)} %add_convert_fusion.1), channel_id=1, source_target_pairs={{0,3},{1,0},{2,1},{3,2},{4,7},{5,4},{6,5},{7,6},{8,11},{9,8},{10,9... | collective-permute-start | bytes 786440 | tf_op jit(solution)/shard_map/ppermute | solution.py:365
  234.0 5.5 %collective-permute-done.29 = bf16[64,2048]{1,0:T(8,128)(2,1)S(1)} collective-permute-done((bf16[64,2048]{1,0:T(8,128)(2,1)S(1)}, bf16[64,2048]{1,0:T(8,128)(2,1)S(1)}, u32[]{:S(2)}, u32[]{:S(2)}) %collective-permute-start.29) | collective-permute-done | bytes 262176 | tf_op jit(solution)/shard_map/ppermute | solution.py:364
  240.5 4.6 %collective-permute-done.27 = bf16[64,2048]{1,0:T(8,128)(2,1)S(1)} collective-permute-done((bf16[64,2048]{1,0:T(8,128)(2,1)S(1)}, bf16[64,2048]{1,0:T(8,128)(2,1)S(1)}, u32[]{:S(2)}, u32[]{:S(2)}) %collective-permute-start.27) | collective-permute-done | bytes 262176 | tf_op jit(solution)/shard_map/ppermute | solution.py:362
  245.2 3.5 %collective-permute-done.23 = bf16[64,2048]{1,0:T(8,128)(2,1)S(1)} collective-permute-done((bf16[64,2048]{1,0:T(8,128)(2,1)S(1)}, bf16[64,2048]{1,0:T(8,128)(2,1)S(1)}, u32[]{:S(2)}, u32[]{:S(2)}) %collective-permute-start.23) | collective-permute-done | bytes 262176 | tf_op jit(solution)/shard_map/ppermute | solution.py:364
  (121 shorter events, 35.0 us)
Async XLA Ops:
  1.4 15.8 %all-to-all-start.2 = ((s32[64,1,12]{2,1,0:T(1,128)}), s32[64,1,12]{2,1,0:T(1,128)S(1)}, u32[]{:S(2)}, u32[]{:S(2)}) async-start(s32[64,1,12]{2,1,0:T(1,128)} %broadcast_in_dim.31), calls=%async_computation.2 | async-start | bytes 65536 | tf_op jit(solution)/shard_map/all_to_all | solution.py:399
  22.8 10.5 %collective-permute-start.10 = (bf16[2,2,2,128,128]{4,3,2,1,0:T(8,128)(2,1)S(1)}, bf16[2,2,2,128,128]{4,3,2,1,0:T(8,128)(2,1)S(1)}, u32[]{:S(2)}, u32[]{:S(2)}) collective-permute-start(bf16[2,2,2,128,128]{4,3,2,1,0:T(8,128)(2,1)S(1)} %get-tuple-element.97), channel_id=1, source_target_pairs={{0,112},{4,116},{8,120},{12,124},{16,0},{20,4},{24,8},{28,12},{32,... | collective-permute-start | bytes 786440 | tf_op jit(solution)/shard_map/ppermute | solution.py:150
  24.5 9.2 %collective-permute-start.6 = (bf16[2,2,2,128,128]{4,3,2,1,0:T(8,128)(2,1)S(1)}, bf16[2,2,2,128,128]{4,3,2,1,0:T(8,128)(2,1)S(1)}, u32[]{:S(2)}, u32[]{:S(2)}) collective-permute-start(bf16[2,2,2,128,128]{4,3,2,1,0:T(8,128)(2,1)S(1)} %get-tuple-element.97), channel_id=1, source_target_pairs={{0,16},{4,20},{8,24},{12,28},{16,32},{20,36},{24,40},{28,44},{32,4... | collective-permute-start | bytes 786440 | tf_op jit(solution)/shard_map/ppermute | solution.py:149
  26.1 12.8 %collective-permute-start.18 = (bf16[2,2,2,128,128]{4,3,2,1,0:T(8,128)(2,1)S(1)}, bf16[2,2,2,128,128]{4,3,2,1,0:T(8,128)(2,1)S(1)}, u32[]{:S(2)}, u32[]{:S(2)}) collective-permute-start(bf16[2,2,2,128,128]{4,3,2,1,0:T(8,128)(2,1)S(1)} %get-tuple-element.98), channel_id=1, source_target_pairs={{0,112},{4,116},{8,120},{12,124},{16,0},{20,4},{24,8},{28,12},{32,... | collective-permute-start | bytes 786440 | tf_op jit(solution)/shard_map/ppermute | solution.py:150
  26.5 12.9 %collective-permute-start.14 = (bf16[2,2,2,128,128]{4,3,2,1,0:T(8,128)(2,1)S(1)}, bf16[2,2,2,128,128]{4,3,2,1,0:T(8,128)(2,1)}, u32[]{:S(2)}, u32[]{:S(2)}) collective-permute-start(bf16[2,2,2,128,128]{4,3,2,1,0:T(8,128)(2,1)S(1)} %get-tuple-element.98), channel_id=1, source_target_pairs={{0,16},{4,20},{8,24},{12,28},{16,32},{20,36},{24,40},{28,44},{32,4... | collective-permute-start | bytes 786440 | tf_op jit(solution)/shard_map/ppermute | solution.py:149
  33.3 11.3 %collective-permute-start.11 = (bf16[2,2,2,128,128]{4,3,2,1,0:T(8,128)(2,1)S(1)}, bf16[2,2,2,128,128]{4,3,2,1,0:T(8,128)(2,1)}, u32[]{:S(2)}, u32[]{:S(2)}) collective-permute-start(bf16[2,2,2,128,128]{4,3,2,1,0:T(8,128)(2,1)S(1)} %collective-permute-done.10), channel_id=1, source_target_pairs={{0,112},{4,116},{8,120},{12,124},{16,0},{20,4},{24,8},{28,12},{32,... | collective-permute-start | bytes 786440 | tf_op jit(solution)/shard_map/ppermute | solution.py:150
  33.6 11.3 %collective-permute-start.7 = (bf16[2,2,2,128,128]{4,3,2,1,0:T(8,128)(2,1)S(1)}, bf16[2,2,2,128,128]{4,3,2,1,0:T(8,128)(2,1)}, u32[]{:S(2)}, u32[]{:S(2)}) collective-permute-start(bf16[2,2,2,128,128]{4,3,2,1,0:T(8,128)(2,1)S(1)} %collective-permute-done.6), channel_id=1, source_target_pairs={{0,16},{4,20},{8,24},{12,28},{16,32},{20,36},{24,40},{28,44},{32,4... | collective-permute-start | bytes 786440 | tf_op jit(solution)/shard_map/ppermute | solution.py:149
  38.9 11.3 %collective-permute-start.19 = (bf16[2,2,2,128,128]{4,3,2,1,0:T(8,128)(2,1)S(1)}, bf16[2,2,2,128,128]{4,3,2,1,0:T(8,128)(2,1)}, u32[]{:S(2)}, u32[]{:S(2)}) collective-permute-start(bf16[2,2,2,128,128]{4,3,2,1,0:T(8,128)(2,1)S(1)} %collective-permute-done.18), channel_id=1, source_target_pairs={{0,112},{4,116},{8,120},{12,124},{16,0},{20,4},{24,8},{28,12},{32,... | collective-permute-start | bytes 786440 | tf_op jit(solution)/shard_map/ppermute | solution.py:150
  39.4 11.2 %collective-permute-start.15 = (bf16[2,2,2,128,128]{4,3,2,1,0:T(8,128)(2,1)}, bf16[2,2,2,128,128]{4,3,2,1,0:T(8,128)(2,1)}, u32[]{:S(2)}, u32[]{:S(2)}) collective-permute-start(bf16[2,2,2,128,128]{4,3,2,1,0:T(8,128)(2,1)} %collective-permute-done.14), channel_id=1, source_target_pairs={{0,16},{4,20},{8,24},{12,28},{16,32},{20,36},{24,40},{28,44},{32,4... | collective-permute-start | bytes 786440 | tf_op jit(solution)/shard_map/ppermute | solution.py:149
  44.6 11.1 %collective-permute-start.12 = (bf16[2,2,2,128,128]{4,3,2,1,0:T(8,128)(2,1)}, bf16[2,2,2,128,128]{4,3,2,1,0:T(8,128)(2,1)S(1)}, u32[]{:S(2)}, u32[]{:S(2)}) collective-permute-start(bf16[2,2,2,128,128]{4,3,2,1,0:T(8,128)(2,1)} %collective-permute-done.11), channel_id=1, source_target_pairs={{0,112},{4,116},{8,120},{12,124},{16,0},{20,4},{24,8},{28,12},{32,... | collective-permute-start | bytes 786440 | tf_op jit(solution)/shard_map/ppermute | solution.py:150
  45.0 11.2 %collective-permute-start.8 = (bf16[2,2,2,128,128]{4,3,2,1,0:T(8,128)(2,1)}, bf16[2,2,2,128,128]{4,3,2,1,0:T(8,128)(2,1)S(1)}, u32[]{:S(2)}, u32[]{:S(2)}) collective-permute-start(bf16[2,2,2,128,128]{4,3,2,1,0:T(8,128)(2,1)} %collective-permute-done.7), channel_id=1, source_target_pairs={{0,16},{4,20},{8,24},{12,28},{16,32},{20,36},{24,40},{28,44},{32,4... | collective-permute-start | bytes 786440 | tf_op jit(solution)/shard_map/ppermute | solution.py:149
  50.2 11.1 %collective-permute-start.20 = (bf16[2,2,2,128,128]{4,3,2,1,0:T(8,128)(2,1)}, bf16[2,2,2,128,128]{4,3,2,1,0:T(8,128)(2,1)S(1)}, u32[]{:S(2)}, u32[]{:S(2)}) collective-permute-start(bf16[2,2,2,128,128]{4,3,2,1,0:T(8,128)(2,1)} %collective-permute-done.19), channel_id=1, source_target_pairs={{0,112},{4,116},{8,120},{12,124},{16,0},{20,4},{24,8},{28,12},{32,... | collective-permute-start | bytes 786440 | tf_op jit(solution)/shard_map/ppermute | solution.py:150
  50.6 11.9 %collective-permute-start.16 = (bf16[2,2,2,128,128]{4,3,2,1,0:T(8,128)(2,1)}, bf16[2,2,2,128,128]{4,3,2,1,0:T(8,128)(2,1)S(1)}, u32[]{:S(2)}, u32[]{:S(2)}) collective-permute-start(bf16[2,2,2,128,128]{4,3,2,1,0:T(8,128)(2,1)} %collective-permute-done.15), channel_id=1, source_target_pairs={{0,16},{4,20},{8,24},{12,28},{16,32},{20,36},{24,40},{28,44},{32,4... | collective-permute-start | bytes 786440 | tf_op jit(solution)/shard_map/ppermute | solution.py:149
  55.8 16.6 %collective-permute-start.13 = (bf16[1,2,2,128,128]{4,3,2,1,0:T(8,128)(2,1)S(1)}, bf16[1,2,2,128,128]{4,3,2,1,0:T(8,128)(2,1)S(1)}, u32[]{:S(2)}, u32[]{:S(2)}) collective-permute-start(bf16[1,2,2,128,128]{4,3,2,1,0:T(8,128)(2,1)S(1)} %slice.99), channel_id=1, source_target_pairs={{0,112},{4,116},{8,120},{12,124},{16,0},{20,4},{24,8},{28,12},{32,... | collective-permute-start | bytes 393224 | tf_op jit(solution)/shard_map/ppermute | solution.py:154
  56.9 15.4 %collective-permute-start.9 = (bf16[1,2,2,128,128]{4,3,2,1,0:T(8,128)(2,1)S(1)}, bf16[1,2,2,128,128]{4,3,2,1,0:T(8,128)(2,1)}, u32[]{:S(2)}, u32[]{:S(2)}) collective-permute-start(bf16[1,2,2,128,128]{4,3,2,1,0:T(8,128)(2,1)S(1)} %slice.98), channel_id=1, source_target_pairs={{0,16},{4,20},{8,24},{12,28},{16,32},{20,36},{24,40},{28,44},{32,4... | collective-permute-start | bytes 393224 | tf_op jit(solution)/shard_map/ppermute | solution.py:153
  62.1 10.3 %collective-permute-start.21 = (bf16[1,2,2,128,128]{4,3,2,1,0:T(8,128)(2,1)S(1)}, bf16[1,2,2,128,128]{4,3,2,1,0:T(8,128)(2,1)}, u32[]{:S(2)}, u32[]{:S(2)}) collective-permute-start(bf16[1,2,2,128,128]{4,3,2,1,0:T(8,128)(2,1)S(1)} %slice.101), channel_id=1, source_target_pairs={{0,112},{4,116},{8,120},{12,124},{16,0},{20,4},{24,8},{28,12},{32,... | collective-permute-start | bytes 393224 | tf_op jit(solution)/shard_map/ppermute | solution.py:154
  63.2 9.1 %collective-permute-start.17 = (bf16[1,2,2,128,128]{4,3,2,1,0:T(8,128)(2,1)S(1)}, bf16[1,2,2,128,128]{4,3,2,1,0:T(8,128)(2,1)}, u32[]{:S(2)}, u32[]{:S(2)}) collective-permute-start(bf16[1,2,2,128,128]{4,3,2,1,0:T(8,128)(2,1)S(1)} %slice.100), channel_id=1, source_target_pairs={{0,16},{4,20},{8,24},{12,28},{16,32},{20,36},{24,40},{28,44},{32,4... | collective-permute-start | bytes 393224 | tf_op jit(solution)/shard_map/ppermute | solution.py:153
  98.1 38.4 %collective-permute-start = (bf16[2,2,2,128,128]{4,3,2,1,0:T(8,128)(2,1)}, bf16[2,2,2,128,128]{4,3,2,1,0:T(8,128)(2,1)S(1)}, u32[]{:S(2)}, u32[]{:S(2)}) collective-permute-start(bf16[2,2,2,128,128]{4,3,2,1,0:T(8,128)(2,1)} %get-tuple-element.69), channel_id=1, source_target_pairs={{0,4},{4,8},{8,12},{12,0},{16,20},{20,24},{24,28},{28,16},{32,36},... | collective-permute-start | bytes 786440 | tf_op jit(solution)/shard_map/cond/branch_1_fun/ppermute | solution.py:418
  98.3 39.1 %collective-permute-start.1 = (bf16[2,2,2,128,128]{4,3,2,1,0:T(8,128)(2,1)}, bf16[2,2,2,128,128]{4,3,2,1,0:T(8,128)(2,1)S(1)}, u32[]{:S(2)}, u32[]{:S(2)}) collective-permute-start(bf16[2,2,2,128,128]{4,3,2,1,0:T(8,128)(2,1)} %get-tuple-element.70), channel_id=1, source_target_pairs={{0,8},{4,12},{8,0},{12,4},{16,24},{20,28},{24,16},{28,20},{32,40},... | collective-permute-start | bytes 786440 | tf_op jit(solution)/shard_map/cond/branch_1_fun/ppermute | solution.py:418
  98.3 39.1 %collective-permute-start.2 = (bf16[2,2,2,128,128]{4,3,2,1,0:T(8,128)(2,1)}, bf16[2,2,2,128,128]{4,3,2,1,0:T(8,128)(2,1)S(1)}, u32[]{:S(2)}, u32[]{:S(2)}) collective-permute-start(bf16[2,2,2,128,128]{4,3,2,1,0:T(8,128)(2,1)} %get-tuple-element.71), channel_id=1, source_target_pairs={{0,12},{4,0},{8,4},{12,8},{16,28},{20,16},{24,20},{28,24},{32,44},... | collective-permute-start | bytes 786440 | tf_op jit(solution)/shard_map/cond/branch_1_fun/ppermute | solution.py:418
  125.8 19.2 %collective-permute-start.3 = (bf16[2,2,2,128,128]{4,3,2,1,0:T(8,128)(2,1)}, bf16[2,2,2,128,128]{4,3,2,1,0:T(8,128)(2,1)S(1)}, u32[]{:S(2)}, u32[]{:S(2)}) collective-permute-start(bf16[2,2,2,128,128]{4,3,2,1,0:T(8,128)(2,1)} %get-tuple-element.82), channel_id=1, source_target_pairs={{0,4},{4,8},{8,12},{12,0},{16,20},{20,24},{24,28},{28,16},{32,36},... | collective-permute-start | bytes 786440 | tf_op jit(solution)/shard_map/cond/branch_1_fun/ppermute | solution.py:418
  136.5 9.5 %collective-permute-start.4 = (bf16[2,2,2,128,128]{4,3,2,1,0:T(8,128)(2,1)}, bf16[2,2,2,128,128]{4,3,2,1,0:T(8,128)(2,1)S(1)}, u32[]{:S(2)}, u32[]{:S(2)}) collective-permute-start(bf16[2,2,2,128,128]{4,3,2,1,0:T(8,128)(2,1)} %get-tuple-element.83), channel_id=1, source_target_pairs={{0,8},{4,12},{8,0},{12,4},{16,24},{20,28},{24,16},{28,20},{32,40},... | collective-permute-start | bytes 786440 | tf_op jit(solution)/shard_map/cond/branch_1_fun/ppermute | solution.py:418
  136.5 11.9 %collective-permute-start.5 = (bf16[2,2,2,128,128]{4,3,2,1,0:T(8,128)(2,1)}, bf16[2,2,2,128,128]{4,3,2,1,0:T(8,128)(2,1)S(1)}, u32[]{:S(2)}, u32[]{:S(2)}) collective-permute-start(bf16[2,2,2,128,128]{4,3,2,1,0:T(8,128)(2,1)} %get-tuple-element.84), channel_id=1, source_target_pairs={{0,12},{4,0},{8,4},{12,8},{16,28},{20,16},{24,20},{28,24},{32,44},... | collective-permute-start | bytes 786440 | tf_op jit(solution)/shard_map/cond/branch_1_fun/ppermute | solution.py:418
  205.9 28.0 %collective-permute-start.30 = (bf16[64,2048]{1,0:T(8,128)(2,1)S(1)}, bf16[64,2048]{1,0:T(8,128)(2,1)S(1)}, u32[]{:S(2)}, u32[]{:S(2)}) collective-permute-start(bf16[64,2048]{1,0:T(8,128)(2,1)S(1)} %slice.83), channel_id=1, source_target_pairs={{0,3},{1,0},{2,1},{3,2},{4,7},{5,4},{6,5},{7,6},{8,11},{9,8},{10,9... | collective-permute-start | bytes 786440 | tf_op jit(solution)/shard_map/ppermute | solution.py:363
  209.0 25.0 %collective-permute-start.33 = (bf16[64,2048]{1,0:T(8,128)(2,1)S(1)}, bf16[64,2048]{1,0:T(8,128)(2,1)S(1)}, u32[]{:S(2)}, u32[]{:S(2)}) collective-permute-start(bf16[64,2048]{1,0:T(8,128)(2,1)S(1)} %slice.87), channel_id=1, source_target_pairs={{0,1},{1,2},{2,3},{3,0},{4,5},{5,6},{6,7},{7,4},{8,9},{9,10},{10,1... | collective-permute-start | bytes 786440 | tf_op jit(solution)/shard_map/ppermute | solution.py:362
  209.0 13.2 %collective-permute-start.28 = (bf16[64,2048]{1,0:T(8,128)(2,1)S(1)}, bf16[64,2048]{1,0:T(8,128)(2,1)S(1)}, u32[]{:S(2)}, u32[]{:S(2)}) collective-permute-start(bf16[64,2048]{1,0:T(8,128)(2,1)S(1)} %get-tuple-element.121), channel_id=1, source_target_pairs={{0,1},{1,2},{2,3},{3,0},{4,5},{5,6},{6,7},{7,4},{8,9},{9,10},{10,1... | collective-permute-start | bytes 786440 | tf_op jit(solution)/shard_map/ppermute | solution.py:360
  209.7 12.7 %collective-permute-start.31 = (bf16[64,2048]{1,0:T(8,128)(2,1)S(1)}, bf16[64,2048]{1,0:T(8,128)(2,1)S(1)}, u32[]{:S(2)}, u32[]{:S(2)}) collective-permute-start(bf16[64,2048]{1,0:T(8,128)(2,1)S(1)} %get-tuple-element.122), channel_id=1, source_target_pairs={{0,3},{1,0},{2,1},{3,2},{4,7},{5,4},{6,5},{7,6},{8,11},{9,8},{10,9... | collective-permute-start | bytes 786440 | tf_op jit(solution)/shard_map/ppermute | solution.py:361
  214.4 26.2 %collective-permute-start.24 = (bf16[64,2048]{1,0:T(8,128)(2,1)S(1)}, bf16[64,2048]{1,0:T(8,128)(2,1)S(1)}, u32[]{:S(2)}, u32[]{:S(2)}) collective-permute-start(bf16[64,2048]{1,0:T(8,128)(2,1)S(1)} %slice.75), channel_id=1, source_target_pairs={{0,3},{1,0},{2,1},{3,2},{4,7},{5,4},{6,5},{7,6},{8,11},{9,8},{10,9... | collective-permute-start | bytes 786440 | tf_op jit(solution)/shard_map/ppermute | solution.py:363
  229.8 9.7 %collective-permute-start.29 = (bf16[64,2048]{1,0:T(8,128)(2,1)S(1)}, bf16[64,2048]{1,0:T(8,128)(2,1)S(1)}, u32[]{:S(2)}, u32[]{:S(2)}) collective-permute-start(bf16[64,2048]{1,0:T(8,128)(2,1)S(1)} %add_convert_fusion.3), channel_id=1, source_target_pairs={{0,1},{1,2},{2,3},{3,0},{4,5},{5,6},{6,7},{7,4},{8,9},{9,10},{10,1... | collective-permute-start | bytes 786440 | tf_op jit(solution)/shard_map/ppermute | solution.py:364
  230.1 10.2 %collective-permute-start.32 = (bf16[64,2048]{1,0:T(8,128)(2,1)S(1)}, bf16[64,2048]{1,0:T(8,128)(2,1)S(1)}, u32[]{:S(2)}, u32[]{:S(2)}) collective-permute-start(bf16[64,2048]{1,0:T(8,128)(2,1)S(1)} %add_convert_fusion.1), channel_id=1, source_target_pairs={{0,3},{1,0},{2,1},{3,2},{4,7},{5,4},{6,5},{7,6},{8,11},{9,8},{10,9... | collective-permute-start | bytes 786440 | tf_op jit(solution)/shard_map/ppermute | solution.py:365
  233.9 11.3 %collective-permute-start.27 = (bf16[64,2048]{1,0:T(8,128)(2,1)S(1)}, bf16[64,2048]{1,0:T(8,128)(2,1)S(1)}, u32[]{:S(2)}, u32[]{:S(2)}) collective-permute-start(bf16[64,2048]{1,0:T(8,128)(2,1)S(1)} %slice.79), channel_id=1, source_target_pairs={{0,1},{1,2},{2,3},{3,0},{4,5},{5,6},{6,7},{7,4},{8,9},{9,10},{10,1... | collective-permute-start | bytes 786440 | tf_op jit(solution)/shard_map/ppermute | solution.py:362
  234.0 14.7 %collective-permute-start.23 = (bf16[64,2048]{1,0:T(8,128)(2,1)S(1)}, bf16[64,2048]{1,0:T(8,128)(2,1)S(1)}, u32[]{:S(2)}, u32[]{:S(2)}) collective-permute-start(bf16[64,2048]{1,0:T(8,128)(2,1)S(1)} %add_convert_fusion.7), channel_id=1, source_target_pairs={{0,1},{1,2},{2,3},{3,0},{4,5},{5,6},{6,7},{7,4},{8,9},{9,10},{10,1... | collective-permute-start | bytes 786440 | tf_op jit(solution)/shard_map/ppermute | solution.py:364
  (22 other events, 401.7 us)
